TPU v7x, 128 devices: a whole 4x4x4 slice. The times are simulated.
128 devices in a mesh: row: 8 (over z_hi, x), tensor: 16 (over z_lo, y, core).
Axes of the slice: x: 4, y: 4, z: 4 (z_hi: 2, z_lo: 2; z = z_hi * 2 + z_lo), core: 2. Of those that a mesh axis runs over, the one named last changes fastest.
Arguments:
- cells: bfloat16 [1024, 4, 4096], P(('row', 'tensor')), may hold values from -6 to 6
- norm1_gain: float32 [4096], replicated, may hold values from 0.25 to 1.75
- w_qkv: bfloat16 [4096, 3, 4096], P(None, None, 'tensor'), may hold values from -0.09375 to 0.09375
- row_bias: float32 [32, 1024, 1024], P('tensor', 'row'), may hold values from -12 to 400
- w_out: bfloat16 [4096, 4096], P('tensor'), may hold values from -0.09375 to 0.09375
- norm2_gain: float32 [4096], replicated, may hold values from 0.25 to 1.75
- w_gate_up: bfloat16 [4096, 2, 11008], P(None, None, 'tensor'), may hold values from -0.09375 to 0.09375
- w_down: bfloat16 [11008, 4096], P('tensor'), may hold values from -0.0546875 to 0.0546875
Outputs:
- state: bfloat16 [1024, 4, 4096], P(('row', 'tensor'))
- result: bfloat16 [1024, 4, 4096], P(('row', 'tensor'))
All inputs are finite; a program needn't handle non-finite values.
Results may differ from a plain program's by a relative error of at most 0.029.
Values may be sent and summed in bfloat16 or wider, within the bound.
A program may use at most 128 MiB of HBM per device.

v0:
```python
import math

import jax
import jax.numpy as jnp
from jax import lax
from jax.sharding import PartitionSpec as P

HD = 128


def normalize(values, gain):
    wide = values.astype(jnp.float32)
    inverse = lax.rsqrt(jnp.mean(wide * wide, axis=-1, keepdims=True) + 1e-05)
    return (wide * inverse * gain).astype(jnp.bfloat16)


def shards(cells, norm1_gain, w_qkv, row_bias, w_out, norm2_gain, w_gate_up, w_down):
    row_local, col_count, width = cells.shape
    heads_local = w_out.shape[0] // HD
    units_local = w_down.shape[0]
    qkv_flat = w_qkv.reshape(width, 3 * heads_local * HD)
    gate_flat = w_gate_up.reshape(width, 2 * units_local)
    piece = lax.all_gather(normalize(cells, norm1_gain), "tensor", axis=0, tiled=True)
    count = piece.shape[0]
    output = jnp.dot(piece.reshape(-1, width), qkv_flat, preferred_element_type=jnp.float32)
    projected = output.astype(jnp.bfloat16).reshape(count, col_count, 3, heads_local, HD)
    queries = projected[:, :, 0]
    keys_local = projected[:, :, 1]
    values_local = projected[:, :, 2]
    block_rows = queries.shape[0]
    products = jnp.einsum(
        "ichd,jchd->chij",
        queries,
        lax.all_gather(keys_local, "row", axis=0, tiled=True),
        preferred_element_type=jnp.float32,
    )
    scores = products * (1.0 / math.sqrt(HD)) + row_bias[None]
    peak = jnp.max(scores, axis=-1, keepdims=True)
    exponent = jnp.exp(scores - peak)
    total = jnp.sum(exponent, axis=-1)
    weights = exponent.astype(jnp.bfloat16)
    summed = jnp.einsum(
        "chij,jchd->ichd",
        weights,
        lax.all_gather(values_local, "row", axis=0, tiled=True),
        preferred_element_type=jnp.float32,
    )
    context = (summed / jnp.transpose(total, (2, 0, 1))[..., None]).astype(jnp.bfloat16)
    context = context.reshape(block_rows, col_count, heads_local * HD)
    slab = context
    output = jnp.dot(slab.reshape(-1, heads_local * HD), w_out, preferred_element_type=jnp.float32)
    attended = lax.psum_scatter(
        output.reshape(row_local * lax.axis_size("tensor"), col_count, width).astype(jnp.bfloat16),
        "tensor",
        scatter_dimension=0,
        tiled=True,
    ).astype(jnp.float32)
    state = (cells.astype(jnp.float32) + attended).astype(jnp.bfloat16)
    piece = lax.all_gather(normalize(state, norm2_gain), "tensor", axis=0, tiled=True)
    count = piece.shape[0]
    gate_up = jnp.dot(piece.reshape(-1, width), gate_flat, preferred_element_type=jnp.float32)
    gate_up = gate_up.reshape(count, col_count, 2, units_local)
    activated = (jax.nn.silu(gate_up[:, :, 0]) * gate_up[:, :, 1]).astype(jnp.bfloat16)
    slab = activated
    output = jnp.dot(slab.reshape(-1, units_local), w_down, preferred_element_type=jnp.float32)
    feed = lax.psum_scatter(
        output.reshape(row_local * lax.axis_size("tensor"), col_count, width).astype(jnp.bfloat16),
        "tensor",
        scatter_dimension=0,
        tiled=True,
    ).astype(jnp.float32)
    result = (state.astype(jnp.float32) + feed).astype(jnp.bfloat16)
    return (state, result)


def solution(mesh):
    in_specs = (
        P(("row", "tensor"), None, None),
        P(),
        P(None, None, "tensor"),
        P("tensor", "row", None),
        P("tensor", None),
        P(),
        P(None, None, "tensor"),
        P("tensor", None),
    )
    out_specs = (P(("row", "tensor"), None, None), P(("row", "tensor"), None, None))
    return jax.shard_map(shards, mesh=mesh, in_specs=in_specs, out_specs=out_specs, check_vma=False)
```

profile of v0, /device:TPU:1, one launch (start us, length us, event | category | flops | bytes accessed | tf_op | source)
XLA Modules:
  0.0 395.8 jit_solution(3421782672515859101)
XLA Ops:
  7.2 0.0 copy-start
  7.2 0.0 all-gather.7.cloned.1.call-start
  7.2 1.5 fusion.39
  8.7 1.8 fusion.41
  10.5 0.0 all-gather.7.cloned.1.call-update
  10.6 0.0 all-gather.13.cloned.1.call-start
  10.6 8.8 %copy.30 = bf16[4096,3,256]{0,2,1:T(8,128)(2,1)} copy(bf16[4096,3,256]{2,0,1:T(8,128)(2,1)} %param.10) | data formatting | bytes 12582912 | tf_op args[2]
  19.4 32.3 %all-gather.7.cloned.1.call-done = bf16[128,4,4096]{2,0,1:T(8,128)(2,1)} async-done(((bf16[8,4,4096]{2,0,1:T(8,128)(2,1)}), bf16[128,4,4096]{2,0,1:T(8,128)(2,1)}) %all-gather.7.cloned.1.call-update) | async-done | bytes 4194320 | tf_op jit(solution)/shard_map/all_gather | solution.py:23
  51.7 7.5 %copy.29 = bf16[128,4,4096]{2,1,0:T(4,128)(2,1)} copy(bf16[128,4,4096]{2,0,1:T(8,128)(2,1)} %all-gather.7.cloned.1.call-done) | data formatting | bytes 8388608 | tf_op jit(solution)/shard_map/all_gather | solution.py:23
  59.2 6.9 %reshape.52 = bf16[512,4096]{1,0:T(8,128)(2,1)} reshape(bf16[128,4,4096]{2,1,0:T(4,128)(2,1)} %copy.29) | data formatting | bytes 8388608 | tf_op jit(solution)/shard_map/reshape | solution.py:25
  66.1 8.4 %convolution_convert_fusion.2 = bf16[512,768]{1,0:T(8,128)(2,1)} fusion(bf16[512,4096]{1,0:T(8,128)(2,1)} %reshape.52, bf16[4096,768]{0,1:T(8,128)(2,1)} %bitcast.79), kind=kOutput, calls=%fused_computation.25 | convolution fusion | flops 3221618688 | bytes 11272192 | tf_op jit(solution)/shard_map/dot_general | solution.py:25
  74.5 2.8 reshape.54
  77.3 2.3 fusion.50
  79.7 0.7 copy.46
  80.4 0.0 all-gather.13.cloned.1.call-update
  80.4 0.0 all-gather.11.cloned.1.call-start
  80.5 1.8 copy.44
  82.3 0.0 all-gather.11.cloned.1.call-update
  82.3 0.2 reduce-scatter.7.cloned.1.call-start
  82.6 51.3 %all-gather.13.cloned.1.call-done = bf16[1024,4,1,2,128]{4,0,3,1,2:T(8,128)(2,1)} async-done(((bf16[128,4,1,2,128]{4,0,3,1,2:T(8,128)(2,1)}), bf16[1024,4,1,2,128]{4,0,3,1,2:T(8,128)(2,1)}) %all-gather.13.cloned.1.call-update) | async-done | bytes 2097168 | tf_op jit(solution)/shard_map/all_gather | solution.py:34
  133.8 0.0 copy-done.3
  133.8 2.4 fusion.8
  136.2 1.9 copy-done.2
  138.2 1.0 fusion.9
  139.2 53.6 %all-gather.11.cloned.1.call-done = bf16[1024,4,1,2,128]{0,4,3,1,2:T(8,128)(2,1)} async-done(((bf16[128,4,1,2,128]{0,4,3,1,2:T(8,128)(2,1)}), bf16[1024,4,1,2,128]{0,4,3,1,2:T(8,128)(2,1)}) %all-gather.11.cloned.1.call-update) | async-done | bytes 2097168 | tf_op jit(solution)/shard_map/all_gather | solution.py:45
  192.7 4.1 %fusion.32 = bf16[128,4,2,128]{0,3,2,1:T(8,128)(2,1)S(1)} fusion(f32[4,2,128,1024]{3,2,1,0:T(8,128)} %copy-done.2, f32[4,2,128]{2,1,0:T(2,128)S(1)} %get-tuple-element.13, f32[2,128,1024]{2,1,0:T(8,128)S(1)} %copy-done.3, bf16[1024,4,1,2,128]{0,4,3,1,2:T(8,128)(2,1)} %all-gather.11.cloned.1.call-done, f32[128,4,2]{0,2,1:T(2,128)S(1)} %bitcast.83), kind=kOutput, calls=%fused_computation.28 | convolution fusion | flops 272891904 | bytes 7610368 | tf_op jit(solution)/shard_map/chij,jchd->ichd/dot_general | solution.py:42
  196.9 0.0 copy-done
  196.9 1.3 fusion.6
  198.2 2.2 copy.48
  200.4 0.0 reduce-scatter.7.cloned.1.call-update
  200.4 0.0 all-gather.9.cloned.1.call-start
  200.5 62.7 %reduce-scatter.7.cloned.1.call-done = bf16[8,16384]{1,0:T(8,128)(2,1)} async-done(((bf16[128,16384]{1,0:T(8,128)(2,1)}), bf16[8,16384]{1,0:T(8,128)(2,1)}) %reduce-scatter.7.cloned.1.call-update) | async-done | bytes 262160
  263.1 0.0 copy-done.4
  263.1 1.4 fusion.43
  264.5 0.0 copy-done.5
  264.5 0.8 fusion.45
  265.3 0.0 all-gather.9.cloned.1.call-update
  265.3 0.0 reduce-scatter.9.cloned.1.call-start
  265.4 40.3 %all-gather.9.cloned.1.call-done = bf16[128,4,4096]{2,0,1:T(8,128)(2,1)} async-done(((bf16[8,4,4096]{2,0,1:T(8,128)(2,1)}), bf16[128,4,4096]{2,0,1:T(8,128)(2,1)}) %all-gather.9.cloned.1.call-update) | async-done | bytes 4194320 | tf_op jit(solution)/shard_map/all_gather | solution.py:59
  305.7 9.7 %fusion = f32[128,4,2,688]{0,3,2,1:T(8,128)S(1)} fusion(bf16[4096,2,688]{0,2,1:T(8,128)(2,1)} %param.14, bf16[128,4,4096]{2,0,1:T(8,128)(2,1)} %all-gather.9.cloned.1.call-done), kind=kOutput, calls=%fused_computation | convolution fusion | flops 5771362304 | bytes 18284544 | tf_op jit(solution)/shard_map/dot_general | solution.py:61
  315.5 6.5 %fusion.3 = bf16[4,16,8,4096]{3,2,1,0:T(8,128)(2,1)S(1)} fusion(bf16[688,4096]{1,0:T(8,128)(2,1)} %param.15, f32[128,4,2,688]{0,3,2,1:T(8,128)S(1)} %fusion), kind=kOutput, calls=%fused_computation.5 | convolution fusion | flops 2889891840 | bytes 12648448 | tf_op jit(solution)/shard_map/dot_general | solution.py:65
  322.0 0.0 copy-start.1
  322.0 2.2 copy.49
  324.2 0.0 reduce-scatter.9.cloned.1.call-update
  324.2 0.9 copy.36
  325.1 61.9 %reduce-scatter.9.cloned.1.call-done = bf16[8,16384]{1,0:T(8,128)(2,1)} async-done(((bf16[128,16384]{1,0:T(8,128)(2,1)}), bf16[8,16384]{1,0:T(8,128)(2,1)}) %reduce-scatter.9.cloned.1.call-update) | async-done | bytes 262160
  387.0 1.0 fusion.46
  388.0 0.9 copy.37
  (7 shorter events, 0.0 us)
Async XLA Ops:
  7.2 189.7 %copy-start = (bf16[256,4096]{1,0:T(8,128)(2,1)S(1)}, bf16[256,4096]{1,0:T(8,128)(2,1)}, u32[]{:S(2)}) copy-start(bf16[256,4096]{1,0:T(8,128)(2,1)} %param.12) | copy-start | bytes 6291460
  7.2 44.5 %all-gather.7.cloned.1.call-start = ((), (), s32[]{:S(2)}) async-start(), calls=%async_computation.2 | async-start | bytes 4456448 | tf_op jit(solution)/shard_map/all_gather | solution.py:23
  10.6 123.3 %all-gather.13.cloned.1.call-start = ((), (), s32[]{:S(2)}) async-start(), calls=%async_computation.5 | async-start | bytes 2359296 | tf_op jit(solution)/shard_map/all_gather | solution.py:34
  74.5 59.3 %copy-start.3 = (f32[2,128,1024]{2,1,0:T(8,128)S(1)}, f32[2,128,1024]{2,1,0:T(8,128)}, u32[]{:S(2)}) copy-start(f32[2,128,1024]{2,1,0:T(8,128)} %param.11) | copy-start | bytes 3145732
  80.4 112.3 %all-gather.11.cloned.1.call-start = ((), (), s32[]{:S(2)}) async-start(), calls=%async_computation.4 | async-start | bytes 2359296 | tf_op jit(solution)/shard_map/all_gather | solution.py:45
  82.3 180.8 %reduce-scatter.7.cloned.1.call-start = ((), (), s32[]{:S(2)}) async-start(), calls=%async_computation.6 | async-start | bytes 4456448
  136.2 2.0 copy-start.2
  200.4 62.7 %copy-start.4 = (bf16[8,4,4096]{2,1,0:T(4,128)(2,1)S(1)}, bf16[8,4,4096]{2,1,0:T(4,128)(2,1)}, u32[]{:S(2)}) copy-start(bf16[8,4,4096]{2,1,0:T(4,128)(2,1)} %param.8) | copy-start | bytes 786436
  200.4 64.1 %copy-start.5 = (f32[4096]{0:T(1024)S(1)}, f32[4096]{0:T(1024)}, u32[]{:S(2)}) copy-start(f32[4096]{0:T(1024)} %param.13) | copy-start | bytes 49156
  200.4 105.3 %all-gather.9.cloned.1.call-start = ((), (), s32[]{:S(2)}) async-start(), calls=%async_computation.3 | async-start | bytes 4456448 | tf_op jit(solution)/shard_map/all_gather | solution.py:59
  265.3 121.7 %reduce-scatter.9.cloned.1.call-start = ((), (), s32[]{:S(2)}) async-start(), calls=%async_computation.7 | async-start | bytes 4456448
  322.0 67.0 %copy-start.1 = (bf16[256,4096]{1,0:T(8,128)(2,1)S(1)}, bf16[256,4096]{1,0:T(8,128)(2,1)}, u32[]{:S(2)}) copy-start(bf16[256,4096]{1,0:T(8,128)(2,1)} %param.12) | copy-start | bytes 6291460
Sparse Core Ops, SparseCore 0:
  10.7 40.9 all-gather.6
  80.6 53.2 all-gather.12
  136.0 56.6 all-gather.10
  200.5 62.5 reduce-scatter.6
  265.5 40.2 all-gather.8
  324.4 62.6 reduce-scatter.8
where the time goes:
time: 400 us; the launch traced here: 396 us
  waiting for transfers between devices  302 us (76%)
  local copies, waits for them, and re-layouts  39.1 us (10%)
  matrix products  32.4 us (8%)
  between operations  14.2 us (4%)
  other arithmetic  7.51 us (2%)
    unnamed x8, waiting for transfers between devices  125 us
    all_gather x1, waiting for transfers between devices, shards(): lax.all_gather(values_local, 'row', axis=0, tiled=True)  53.6 us
    all_gather x1, waiting for transfers between devices, shards(): lax.all_gather(keys_local, 'row', axis=0, tiled=True)  51.3 us
    all_gather x1, waiting for transfers between devices, shards(): lax.all_gather(normalize(state, norm2_gain), 'tensor', axis=0, tiled=True)  40.3 us
    all_gather x1, waiting for transfers between devices, shards(): lax.all_gather(normalize(cells, norm1_gain), 'tensor', axis=0, tiled=True)  32.3 us
    unnamed x19, local copies, waits for them, and re-layouts  19.6 us
    dot_general x1, matrix products, shards(): jnp.dot(piece.reshape(-1, width), gate_flat, preferred_element_type=jnp.f...  9.71 us
    dot_general x1, matrix products, shards(): jnp.dot(piece.reshape(-1, width), qkv_flat, preferred_element_type=jnp.fl...  8.4 us
  transfers between devices with their start and end apart: 6, of which 6 were waited for; matrix products, arithmetic and copies ran while one was open for 4% of the time, Pallas kernels for 0%

commit v1 on v0

v1 whole, which is shorter than its diff:
```python
import functools
import math

import jax
import jax.numpy as jnp
from jax import lax
from jax.experimental import pallas as pl
from jax.experimental.pallas import tpu as pltpu
from jax.sharding import PartitionSpec as P

MESH = pl.DeviceIdType.MESH
F32 = jnp.float32
BF16 = jnp.bfloat16
D = 4096
UNITS = 688
UPAD = 768
SCALE = 1.0 / math.sqrt(128)

S_BIAS = 0
S_X = 3
S_ZH = 6
S_CTX = 10
S_AG = 13
AG_YA, AG_YB, AG_YBP, AG_ZA, AG_ZB, AG_CO, AG_C = 13, 16, 19, 22, 26, 27, 28
S_RS = 42
RS_C, RS_ZA, RS_YA, RS_YB, RS_ZB = 42, 50, 54, 57, 63
N_SEM = 64


def rows(start, count):
    return pl.ds(pl.multiple_of(start, 16), count)


def normalize(values, gain):
    wide = values.astype(F32)
    inverse = lax.rsqrt(jnp.mean(wide * wide, axis=-1, keepdims=True) + 1e-05)
    return (wide * inverse * gain).astype(BF16)


def layer(cells, gain1, wqkv_hbm, bias_hbm, wout_hbm, gain2, wgu_hbm, wdown_hbm, state, result,
          wq, wo, wg, wd, G, PT, RC, RZA, RYA, RYB, RZB, BV, QB, XR, ZR, CS, CH, ACT, ssem, rsem, lsem):
    r = lax.axis_index("row")
    t = lax.axis_index("tensor")
    zh, x = r // 4, lax.rem(r, 4)
    k, c = t // 2, lax.rem(t, 2)
    zl, y = k // 4, lax.rem(k, 4)
    head, pair = x // 2, lax.rem(x, 2)

    def m4(v):
        return lax.rem(v + 4, 4)

    def tensor_dev(zl_, y_, c_):
        return (r, zl_ * 8 + y_ * 2 + c_)

    sib = tensor_dev(zl, y, 1 - c)
    zpart = tensor_dev(1 - zl, y, c)
    ydev = {d: tensor_dev(zl, m4(y + d), c) for d in (1, 2, 3)}
    xdev = {d: (zh * 4 + m4(x + d), t) for d in (1, 2, 3)}
    zhpart = ((1 - zh) * 4 + x, t)

    def piece(zl_, y_, c_):
        return c_ * 8 + zl_ * 4 + y_

    def rcopy(src, dst, slot, dev):
        return pltpu.make_async_remote_copy(
            src_ref=src, dst_ref=dst, send_sem=ssem.at[slot], recv_sem=rsem.at[slot],
            device_id=dev, device_id_type=MESH)

    own_bias = pltpu.make_async_copy(bias_hbm.at[head], BV.at[x], lsem.at[0])
    fetch_q = pltpu.make_async_copy(wqkv_hbm, wq, lsem.at[1])
    fetch_o = pltpu.make_async_copy(wout_hbm, wo, lsem.at[2])
    fetch_g = pltpu.make_async_copy(wgu_hbm, wg.at[:, pl.ds(0, UNITS)], lsem.at[3])
    fetch_d = pltpu.make_async_copy(wdown_hbm, wd.at[pl.ds(0, UNITS)], lsem.at[4])
    fetch_q.start()

    barrier = pltpu.get_barrier_semaphore()
    peers = [sib, zpart, zhpart] + [ydev[d] for d in (1, 2, 3)] + [xdev[d] for d in (1, 2, 3)]
    for dev in peers:
        pl.semaphore_signal(barrier, inc=1, device_id=dev, device_id_type=MESH)

    me = piece(zl, y, c)
    for part in range(2):
        G[rows(me * 32 + part * 16, 16), :] = normalize(cells[part * 16:(part + 1) * 16, :], gain1[...])

    pl.semaphore_wait(barrier, len(peers))

    def half(p, h):
        return G.at[rows(p * 32 + h * 16, 16)]

    def gather():
        sends = []

        def send(src, slot, dev):
            cp = rcopy(src, src, slot, dev)
            cp.start()
            sends.append(cp)
            return cp

        zb = send(half(me, 1), AG_ZB, zpart)
        ya = {d: send(half(me, 0), AG_YA + d - 1, ydev[d]) for d in (1, 3, 2)}
        za = {0: send(half(me, 0), AG_ZA, zpart)}
        yb = {d: send(half(me, 1), AG_YB + d - 1, ydev[d]) for d in (1, 3, 2)}
        co = send(G.at[rows(me * 32, 32)], AG_CO, sib)
        count = [0]
        shared = []

        def share(p, h):
            shared.append(send(half(p, h), AG_C + count[0], sib))
            count[0] += 1

        zb.wait_recv()
        other = piece(1 - zl, y, c)
        ybp = {d: send(half(other, 1), AG_YBP + d - 1, ydev[d]) for d in (1, 3, 2)}
        share(other, 1)
        for d in (1, 3, 2):
            ya[d].wait_recv()
            p = piece(zl, m4(y - d), c)
            za[d] = send(half(p, 0), AG_ZA + d, zpart)
            share(p, 0)
        za[0].wait_recv()
        share(other, 0)
        for d in (1, 3, 2):
            yb[d].wait_recv()
            share(piece(zl, m4(y - d), c), 1)
        for d in (1, 3, 2):
            za[d].wait_recv()
            share(piece(1 - zl, m4(y - d), c), 0)
        for d in (1, 3, 2):
            ybp[d].wait_recv()
            share(piece(1 - zl, m4(y - d), c), 1)
        co.wait_recv()
        for cp in shared:
            cp.wait_recv()
        for cp in sends:
            cp.wait_send()

    def scatter(finish):
        sends = []

        def send(src, dst, slot, dev):
            cp = rcopy(src, dst, slot, dev)
            cp.start()
            sends.append(cp)
            return cp

        def zside(zrel):
            return zl if zrel == 0 else 1 - zl

        order = [(1, 1), (1, 3), (1, 2), (1, 0), (0, 1), (0, 3), (0, 2), (0, 0)]
        cs = {}
        for zrel, d in order:
            p = piece(zside(zrel), m4(y + d), 1 - c)
            cs[zrel, d] = send(PT.at[rows(p * 32, 32)], RC.at[zrel * 4 + d], RS_C + zrel * 4 + d, sib)
        za, ya, yb = {}, {}, {}
        for zrel, d in order:
            cs[zrel, d].wait_recv()
            p = piece(zside(zrel), m4(y + d), c)
            slot = RC.at[zrel * 4 + d]
            slot[...] = (slot[...].astype(F32) + PT[rows(p * 32, 32), :].astype(F32)).astype(BF16)
            if zrel == 1:
                za[d] = send(slot.at[pl.ds(0, 16)], RZA.at[d], RS_ZA + d, zpart)
            if d:
                yb[zrel, d] = send(slot.at[pl.ds(16, 16)], RYB.at[zrel, d - 1], RS_YB + zrel * 3 + d - 1, ydev[d])
        for d in (1, 3, 2):
            za[d].wait_recv()
            slot = RC.at[d, pl.ds(0, 16)]
            slot[...] = (slot[...].astype(F32) + RZA[d].astype(F32)).astype(BF16)
            ya[d] = send(slot, RYA.at[d - 1], RS_YA + d - 1, ydev[d])
        total = {}
        for zrel in (1, 0):
            for d in (1, 3, 2):
                yb[zrel, d].wait_recv()
            slot = RC.at[zrel * 4, pl.ds(16, 16)]
            sums = slot[...].astype(F32)
            for d in (1, 2, 3):
                sums = sums + RYB[zrel, d - 1].astype(F32)
            if zrel == 1:
                slot[...] = sums.astype(BF16)
                zb = send(slot, RZB, RS_ZB, zpart)
            else:
                total[1] = sums
        za[0].wait_recv()
        for d in (1, 3, 2):
            ya[d].wait_recv()
        sums = RC[0, 0:16].astype(F32) + RZA[0].astype(F32)
        for d in (1, 2, 3):
            sums = sums + RYA[d - 1].astype(F32)
        finish(0, sums)
        zb.wait_recv()
        finish(1, total[1] + RZB[...].astype(F32))
        for cp in sends:
            cp.wait_send()

    own_bias.start()
    bias_copies = []
    for d in (1, 3, 2):
        cp = rcopy(bias_hbm.at[m4(x + d) // 2], BV.at[x], S_BIAS + d - 1, xdev[d])
        cp.start()
        bias_copies.append(cp)
    gather()
    fetch_q.wait()
    fetch_o.start()
    fetch_g.start()
    fetch_d.start()

    @pl.loop(0, 2)
    def _(m):
        lhs = jnp.concatenate([G[rows(m * 128, 128), :], G[rows(256 + m * 128, 128), :]], axis=0)
        for j in range(3):
            acc = jnp.dot(lhs, wq[j], preferred_element_type=F32).reshape(2, 4, 4, 8, 256)
            for col in range(4):
                both = jnp.concatenate([acc[:1, :, col], acc[1:, :, col]], axis=0)
                tiles = [both[cc, kk] for kk in range(4) for cc in range(2)]
                val = jnp.concatenate(tiles, axis=0).astype(BF16)
                for h in range(2):
                    QB[h, col, rows(m * 64, 64), j * 128:(j + 1) * 128] = val[:, h * 128:(h + 1) * 128]

    xc = {}
    for d in (1, 3, 2):
        peer = m4(x + d)
        xc[d] = rcopy(QB.at[peer // 2, pl.ds(lax.rem(peer, 2) * 2, 2)], XR.at[x], S_X + d - 1, xdev[d])
        xc[d].start()
    own_x = pltpu.make_async_copy(QB.at[head, pl.ds(pair * 2, 2)], XR.at[x], lsem.at[5])
    own_x.start()
    wg[:, UNITS:UPAD, :] = jnp.zeros((2, UPAD - UNITS, D), BF16)
    wd[UNITS:UPAD, :] = jnp.zeros((UPAD - UNITS, D), BF16)
    own_x.wait()
    zc = {}
    for d in (0, 1, 3, 2):
        if d:
            xc[d].wait_recv()
        src = m4(x - d)
        zc[d] = rcopy(XR.at[src, :, :, pl.ds(128, 256)], ZR.at[src], S_ZH + d, zhpart)
        zc[d].start()
    own_bias.wait()
    for cp in bias_copies:
        cp.wait_recv()
    for d in range(4):
        zc[d].wait_recv()

    near, far = pl.multiple_of(zh * 512, 512), pl.multiple_of((1 - zh) * 512, 512)
    ctx = {}
    for d in (1, 3, 2, 0):
        block = m4(x + d)
        heads_out = []
        for col in range(2):
            q = XR[block, col, :, 0:128]
            k1 = XR[:, col, :, 128:256].reshape(512, 128)
            k2 = ZR[:, col, :, 0:128].reshape(512, 128)
            dims = (((1,), (1,)), ((), ()))
            s1 = lax.dot_general(q, k1, dims, preferred_element_type=F32) * SCALE + BV[block, :, pl.ds(near, 512)]
            s2 = lax.dot_general(q, k2, dims, preferred_element_type=F32) * SCALE + BV[block, :, pl.ds(far, 512)]
            peak = jnp.maximum(jnp.max(s1, axis=-1, keepdims=True), jnp.max(s2, axis=-1, keepdims=True))
            e1, e2 = jnp.exp(s1 - peak), jnp.exp(s2 - peak)
            total = jnp.sum(e1, axis=-1, keepdims=True) + jnp.sum(e2, axis=-1, keepdims=True)
            v1 = XR[:, col, :, 256:384].reshape(512, 128)
            v2 = ZR[:, col, :, 128:256].reshape(512, 128)
            out = jnp.dot(e1.astype(BF16), v1, preferred_element_type=F32)
            out = out + jnp.dot(e2.astype(BF16), v2, preferred_element_type=F32)
            heads_out.append((out / total).reshape(8, 2, 8, 128))
        tiles = [heads_out[col][kk, cc] for cc in range(2) for kk in range(8) for col in range(2)]
        CS[block] = jnp.concatenate(tiles, axis=0).astype(BF16).reshape(16, 16, 128)
        if d:
            ctx[d] = rcopy(CS.at[block], CH.at[head, :, pair], S_CTX + d - 1, xdev[d])
        else:
            ctx[d] = pltpu.make_async_copy(CS.at[block], CH.at[head, :, pair], lsem.at[6])
        ctx[d].start()
    fetch_o.wait()
    ctx[0].wait()
    for d in (1, 3, 2):
        ctx[d].wait_recv()

    @pl.loop(0, 8)
    def _(n):
        lhs = jnp.concatenate([CH[0].reshape(512, 128), CH[1].reshape(512, 128)], axis=1)
        span = pl.ds(pl.multiple_of(n * 512, 512), 512)
        PT[:, span] = jnp.dot(lhs, wo[:, span], preferred_element_type=F32).astype(BF16)

    def add_attended(h, sums):
        part = slice(h * 16, (h + 1) * 16)
        state[part, :] = (cells[part, :].astype(F32) + sums).astype(BF16)
        G[rows(me * 32 + h * 16, 16), :] = normalize(state[part, :], gain2[...])

    scatter(add_attended)
    gather()
    fetch_g.wait()
    fetch_d.wait()

    @pl.loop(0, 3)
    def _(n):
        span = rows(n * 256, 256)
        dims = (((1,), (1,)), ((), ()))
        for m in range(2):
            lhs = G[m * 256:(m + 1) * 256, :]
            gate = lax.dot_general(lhs, wg[0, span, :], dims, preferred_element_type=F32)
            up = lax.dot_general(lhs, wg[1, span, :], dims, preferred_element_type=F32)
            ACT[m * 256:(m + 1) * 256, pl.ds(pl.multiple_of(n * 256, 256), 256)] = (
                gate / (1.0 + jnp.exp(-gate)) * up).astype(BF16)

    @pl.loop(0, 8)
    def _(n):
        span = pl.ds(pl.multiple_of(n * 512, 512), 512)
        PT[:, span] = jnp.dot(ACT[...], wd[:, span], preferred_element_type=F32).astype(BF16)

    def add_feed(h, sums):
        part = slice(h * 16, (h + 1) * 16)
        result[part, :] = (state[part, :].astype(F32) + sums).astype(BF16)

    scatter(add_feed)
    for cp in bias_copies:
        cp.wait_send()
    for d in (1, 2, 3):
        xc[d].wait_send()
        ctx[d].wait_send()
    for d in range(4):
        zc[d].wait_send()


def shards(cells, norm1_gain, w_qkv, row_bias, w_out, norm2_gain, w_gate_up, w_down):
    own = cells.transpose(1, 0, 2).reshape(32, D)
    vmem = pl.BlockSpec(memory_space=pltpu.VMEM)
    hbm = pl.BlockSpec(memory_space=pl.ANY)
    out = jax.ShapeDtypeStruct((32, D), BF16)
    state, result = pl.pallas_call(
        layer,
        out_shape=(out, out),
        in_specs=[vmem, vmem, hbm, hbm, hbm, vmem, hbm, hbm],
        out_specs=(vmem, vmem),
        scratch_shapes=[
            pltpu.VMEM((3, D, 256), BF16),
            pltpu.VMEM((256, D), BF16),
            pltpu.VMEM((2, UPAD, D), BF16),
            pltpu.VMEM((UPAD, D), BF16),
            pltpu.VMEM((512, D), BF16),
            pltpu.VMEM((512, D), BF16),
            pltpu.VMEM((8, 32, D), BF16),
            pltpu.VMEM((4, 16, D), BF16),
            pltpu.VMEM((3, 16, D), BF16),
            pltpu.VMEM((2, 3, 16, D), BF16),
            pltpu.VMEM((16, D), BF16),
            pltpu.VMEM((4, 128, 1024), F32),
            pltpu.VMEM((2, 4, 128, 384), BF16),
            pltpu.VMEM((4, 2, 128, 384), BF16),
            pltpu.VMEM((4, 2, 128, 256), BF16),
            pltpu.VMEM((4, 16, 16, 128), BF16),
            pltpu.VMEM((2, 16, 2, 16, 128), BF16),
            pltpu.VMEM((512, UPAD), BF16),
            pltpu.SemaphoreType.DMA((N_SEM,)),
            pltpu.SemaphoreType.DMA((N_SEM,)),
            pltpu.SemaphoreType.DMA((8,)),
        ],
        compiler_params=pltpu.CompilerParams(
            collective_id=0, has_side_effects=True, vmem_limit_bytes=60 * 2**20),
        name="layer",
    )(own, norm1_gain.reshape(1, D), w_qkv.transpose(1, 0, 2), row_bias, w_out,
      norm2_gain.reshape(1, D), w_gate_up.transpose(1, 2, 0), w_down)
    return tuple(v.reshape(4, 8, D).transpose(1, 0, 2) for v in (state, result))


def solution(mesh):
    in_specs = (
        P(("row", "tensor"), None, None),
        P(),
        P(None, None, "tensor"),
        P("tensor", "row", None),
        P("tensor", None),
        P(),
        P(None, None, "tensor"),
        P("tensor", None),
    )
    out_specs = (P(("row", "tensor"), None, None), P(("row", "tensor"), None, None))
    return jax.shard_map(shards, mesh=mesh, in_specs=in_specs, out_specs=out_specs, check_vma=False)
```

time: 400 us -> 139 us (0.35)
  waiting for transfers between devices: 302 us -> 0 us
  Pallas kernels: 0 us -> 134 us
  local copies, waits for them, and re-layouts: 39.1 us -> 4.03 us
  matrix products: 32.4 us -> 0 us
  between operations: 14.2 us -> 0.64 us
  other arithmetic: 7.51 us -> 0 us
    all_gather x4 -> x0, waiting for transfers between devices: 178 us -> none  [the longest x1 53.6 us: shards(): lax.all_gather(values_local, 'row', axis=0, tiled=True)]
    pallas_call x0 -> x1, Pallas kernels: none -> 134 us  [shards(): pl.pallas_call(layer, out_shape=(out, out), in_specs=[vmem, vmem, hbm, hb...]
    unnamed x8 -> x0, waiting for transfers between devices: 125 us -> none
    dot_general x6 -> x0, matrix products: 32.4 us -> none  [the longest x1 9.71 us: shards(): jnp.dot(piece.reshape(-1, width), gate_flat, preferred_element_type=jnp.f...]
    unnamed x19 -> x0, local copies, waits for them, and re-layouts: 19.6 us -> none
    reshape x2 -> x0, local copies, waits for them, and re-layouts: 9.72 us -> none  [the longest x1 6.92 us: shards(): piece.reshape(-1, width)]
    all_gather x1 -> x0, local copies, waits for them, and re-layouts: 7.49 us -> none  [shards(): lax.all_gather(normalize(cells, norm1_gain), 'tensor', axis=0, tiled=True)]
    transpose x0 -> x2, local copies, waits for them, and re-layouts: none -> 4.03 us  [the longest x1 2.23 us: shards(): v.reshape(4, 8, D).transpose(1, 0, 2)]
  transfers between devices with their start and end apart: 6 -> 0, of which waited for: 6 -> 0; matrix products, arithmetic and copies ran while one was open for 4% -> 0% of each run, Pallas kernels for 0% -> 0%
where the time goes in v1:
time: 139 us
  Pallas kernels  134 us (96%)
  local copies, waits for them, and re-layouts  4.03 us (3%)
    pallas_call x1, Pallas kernels, shards(): pl.pallas_call(layer, out_shape=(out, out), in_specs=[vmem, vmem, hbm, hb...  134 us

profile of v1, /device:TPU:1, one launch (start us, length us, event | category | flops | bytes accessed | tf_op | source)
XLA Modules:
  0.0 138.6 jit_solution(9253868006271920701)
XLA Ops:
  0.6 1.8 %copy.16 = bf16[4,8,4096]{2,1,0:T(8,128)(2,1)} copy(bf16[4,8,4096]{2,0,1:T(4,128)(2,1)} %bitcast.17) | data formatting | bytes 524288 | tf_op jit(solution)/shard_map/transpose | solution.py:320
  2.4 133.9 %layer.1 = (bf16[32,4096]{1,0:T(8,128)(2,1)}, bf16[32,4096]{1,0:T(8,128)(2,1)}) custom-call(bf16[32,4096]{1,0:T(8,128)(2,1)} %bitcast.16, f32[1,4096]{1,0:T(1,128)} %bitcast.20, bf16[3,4096,256]{2,1,0:T(8,128)(2,1)} %bitcast.15, f32[2,128,1024]{2,1,0:T(8,128)} %bias_hbm.1, bf16[256,4096]{1,0:T(8,128)(2,1)} %wout_hbm.1, f32[1,4096]{1,0:T(1,128)} %bitcast.21, ...), custom_call_target="tpu_custom_call" | custom-call | tf_op jit(solution)/shard_map/layer/pallas_call | solution.py:324
  136.4 2.2 %copy_bitcast_fusion = (bf16[8,4,4096]{2,1,0:T(4,128)(2,1)}, bf16[8,4,4096]{2,1,0:T(4,128)(2,1)}) fusion(bf16[4,8,4096]{2,1,0:T(8,128)(2,1)} %bitcast.19, bf16[4,8,4096]{2,1,0:T(8,128)(2,1)} %bitcast.18), kind=kLoop, calls=%fused_computation | loop fusion | bytes 1048576 | tf_op jit(solution)/shard_map/transpose | solution.py:357

commit v2 on v0

v2 whole, which is shorter than its diff:
```python
import functools
import math

import jax
import jax.numpy as jnp
from jax import lax
from jax.experimental import pallas as pl
from jax.experimental.pallas import tpu as pltpu
from jax.sharding import PartitionSpec as P

MESH = pl.DeviceIdType.MESH
F32 = jnp.float32
BF16 = jnp.bfloat16
D = 4096
UNITS = 688
UPAD = 768
SCALE = 1.0 / math.sqrt(128)

S_BIAS, S_X, S_ZH, S_ZQ, S_CTX = 0, 3, 9, 17, 21
AG_Z, AG_Y, AG_FWD, AG_OWN, AG_NEAR, AG_FAR = 29, 39, 43, 47, 49, 57
RS_C, RS_Z, RS_Y, RS_FWD = 67, 83, 91, 95
N_SEM = 99


def rows(start, count):
    return pl.ds(pl.multiple_of(start, 16), count)


def normalize(values, gain):
    wide = values.astype(F32)
    inverse = lax.rsqrt(jnp.mean(wide * wide, axis=-1, keepdims=True) + 1e-05)
    return (wide * inverse * gain).astype(BF16)


def layer(cells, gain1, wqkv_hbm, bias_hbm, wout_hbm, gain2, wgu_hbm, wdown_hbm, state, result,
          wq, wo, wg, wd, G, PT, RC, RZ, RY, RF, BV, QB, XR, CS, CH, ACT, ssem, rsem, lsem):
    r = lax.axis_index("row")
    t = lax.axis_index("tensor")
    zh, x = r // 4, lax.rem(r, 4)
    k, c = t // 2, lax.rem(t, 2)
    zl, y = k // 4, lax.rem(k, 4)

    def m4(v):
        return lax.rem(v + 4, 4)

    def role(x_):
        turn = m4(x_ + c)
        return turn // 2, lax.rem(turn, 2)

    head, pair = role(x)

    def dev(zh_=zh, x_=x, zl_=zl, y_=y, c_=c):
        return (zh_ * 4 + x_, zl_ * 8 + y_ * 2 + c_)

    sib = dev(c_=1 - c)
    zdev = (dev(zl_=1 - zl), dev(zh_=1 - zh, zl_=1 - zl))
    ydev = {d: dev(y_=m4(y + d)) for d in (1, 2, 3)}
    xdev = {d: dev(x_=m4(x + d)) for d in (1, 2, 3)}
    zhpart = dev(zh_=1 - zh)

    def piece(ref, zl_, h, c_, y_):
        return ref.at[rows((zl_ * 16 + h * 8 + c_ * 4 + y_) * 16, 16)]

    def rcopy(src, dst, slot, target):
        return pltpu.make_async_remote_copy(
            src_ref=src, dst_ref=dst, send_sem=ssem.at[slot], recv_sem=rsem.at[slot],
            device_id=target, device_id_type=MESH)

    def fetch(pairs, slot):
        return [pltpu.make_async_copy(src, dst, lsem.at[slot + i]) for i, (src, dst) in enumerate(pairs)]

    own_bias = pltpu.make_async_copy(bias_hbm.at[head], BV.at[x], lsem.at[0])
    fetch_q = fetch([(wqkv_hbm.at[j, pl.ds(i * 1024, 1024)], wq.at[j, pl.ds(i * 1024, 1024)])
                     for j in range(3) for i in range(4)], 8)
    fetch_o = fetch([(wout_hbm.at[pl.ds(i * 64, 64)], wo.at[pl.ds(i * 64, 64)]) for i in range(4)], 20)
    fetch_g = fetch([(wgu_hbm.at[j, pl.ds(i * 176, w)], wg.at[j, pl.ds(i * 176, w)])
                     for i, w in enumerate((176, 176, 176, 160)) for j in range(2)], 24)
    fetch_d = fetch([(wdown_hbm.at[pl.ds(i * 176, w)], wd.at[pl.ds(i * 176, w)])
                     for i, w in enumerate((176, 176, 176, 160))], 32)

    def start(copies):
        for cp in copies:
            cp.start()

    def wait(copies):
        for cp in copies:
            cp.wait()

    start(fetch_q)

    barrier = pltpu.get_barrier_semaphore()
    peers = [sib, zdev[0], zdev[1], zhpart] + [ydev[d] for d in (1, 2, 3)] + [xdev[d] for d in (1, 2, 3)]
    peers += [dev(zh_=1 - zh, x_=m4(x + d)) for d in (1, 2, 3)]
    for target in peers:
        pl.semaphore_signal(barrier, inc=1, device_id=target, device_id_type=MESH)

    for h in range(2):
        piece(G, zl, h, c, y)[...] = normalize(cells[h * 16:(h + 1) * 16, :], gain1[...])

    pl.semaphore_wait(barrier, len(peers))

    low, high = pl.ds(0, D // 2), pl.ds(D // 2, D // 2)

    def gather(middle):
        sends = []

        def send(ref, slot, target):
            cp = rcopy(ref, ref, slot, target)
            cp.start()
            sends.append(cp)
            return cp

        def mine(h):
            return piece(G, zl, h, c, y)

        zs, ys, near, far = {}, {}, [], []

        def hop(h, d):
            ys[h, d] = send(mine(h), AG_Y + h * 2 + d // 2, ydev[d])

        def arrive(h, d):
            ys[h, d].wait_recv()
            src = piece(G, zl, h, c, m4(y - d))
            zs[h, d] = send(src, AG_Z + h * 5 + d // 2 + 1, zdev[h])
            near.append(send(src, AG_NEAR + h * 4 + d // 2, sib))

        hop(0, 1)
        hop(1, 3)
        for h in range(2):
            zs[h, 0] = send(mine(h), AG_Z + h * 5, zdev[h])
            near.append(send(mine(h), AG_OWN + h, sib))
        arrive(0, 1)
        hop(1, 1)
        arrive(1, 3)
        hop(0, 3)
        fwd = {}

        def forward(h, d):
            lanes = low if d == 1 else high
            fwd[h, d] = send(piece(G, zl, h, c, m4(y - d)).at[:, lanes], AG_FWD + h * 2 + d // 2, ydev[d])

        arrive(1, 1)
        forward(0, 1)
        forward(1, 1)
        arrive(0, 3)
        forward(1, 3)
        forward(0, 3)
        for d in (1, 3):
            for h in range(2):
                fwd[h, d].wait_recv()
                src = piece(G, zl, h, c, m4(y + 2)).at[:, low if d == 1 else high]
                zs[h, d + 3] = send(src, AG_Z + h * 5 + 3 + d // 2, zdev[h])
                near.append(send(src, AG_NEAR + h * 4 + 2 + d // 2, sib))
        for cp in near:
            cp.wait_recv()
        middle()
        for i, d in enumerate((0, 1, 3, 4, 6)):
            for h in range(2):
                zs[h, d].wait_recv()
                src = piece(G, 1 - zl, h, c, m4(y - d if d < 4 else y + 2))
                if d > 3:
                    src = src.at[:, low if d == 4 else high]
                far.append(send(src, AG_FAR + h * 5 + i, sib))
        for cp in far:
            cp.wait_recv()
        for cp in sends:
            cp.wait_send()

    def scatter(produce, finish):
        sends = []

        def send(src, dst, slot, target):
            cp = rcopy(src, dst, slot, target)
            cp.start()
            sends.append(cp)
            return cp

        def add(slot, *others):
            total = slot[...].astype(F32)
            for other in others:
                total = total + other[...].astype(F32)
            slot[...] = total.astype(BF16)

        order = [(h, d) for d in (2, 1, 3, 0) for h in range(2)]
        cs, zs, ys, fwd = {}, {}, {}, {}

        def share(zrel):
            side = zl if zrel == 0 else 1 - zl
            for h, d in order:
                cs[h, d] = send(piece(PT, side, h, 1 - c, m4(y + d)), RC.at[zrel, h, d],
                                RS_C + zrel * 8 + h * 4 + d, sib)

        def pair_up(zrel, h, d):
            cs[h, d].wait_recv()
            add(RC.at[zrel, h, d], piece(PT, zl if zrel == 0 else 1 - zl, h, c, m4(y + d)))

        def cross(h, d):
            zs[h, d] = send(RC.at[1, h, d], RZ.at[h, d], RS_Z + h * 4 + d, zdev[h])

        produce(1 - zl)
        share(1)
        for h in range(2):
            pair_up(1, h, 2)
            cross(h, 2)
        for h, d in order[2:]:
            pair_up(1, h, d)
        cross(0, 1)
        cross(1, 3)
        produce(zl)
        share(0)
        for h in range(2):
            zs[h, 2].wait_send()
            cross(h, 3 if h == 0 else 1)
        for h in range(2):
            pair_up(0, h, 2)
            zs[h, 2].wait_recv()
            add(RC.at[0, h, 2], RZ.at[h, 2])
            for d, lanes in ((1, low), (3, high)):
                fwd[h, d] = send(RC.at[0, h, 2, :, lanes], RF.at[h, d // 2], RS_FWD + h * 2 + d // 2, ydev[d])
        for h, d in order[2:]:
            pair_up(0, h, d)
        for h in range(2):
            zs[h, 1 if h == 0 else 3].wait_send()
            cross(h, 0)
        for h, d in ((0, 1), (1, 3), (0, 3), (1, 1)):
            fwd[h, d].wait_recv()
            zs[h, d].wait_recv()
            first, second = (low, high) if d == 1 else (high, low)
            slot = RC.at[0, h, d]
            add(slot.at[:, first], RZ.at[h, d, :, first], RF.at[h, d // 2])
            add(slot.at[:, second], RZ.at[h, d, :, second])
            ys[h, d] = send(slot, RY.at[h, d // 2], RS_Y + h * 2 + d // 2, ydev[d])
        for h in range(2):
            zs[h, 0].wait_recv()
            sums = RC[0, h, 0].astype(F32) + RZ[h, 0].astype(F32)
            for d in (1, 3):
                ys[h, d].wait_recv()
                sums = sums + RY[h, d // 2].astype(F32)
            finish(h, sums)
        for cp in sends:
            if not any(cp is done for done in (zs[0, 2], zs[1, 2], zs[0, 1], zs[1, 3])):
                cp.wait_send()

    own_bias.start()
    bias_copies = {d: rcopy(bias_hbm.at[role(m4(x + d))[0]], BV.at[x], S_BIAS + d - 1, xdev[d]) for d in (1, 2, 3)}
    bias_copies[1].start()
    bias_copies[3].start()

    xc, own_x = {}, {}

    def place(zh_, zl_, pair_, part):
        return zh_ + pair_ * lax.rem(zl_ + part, 2) * (1 - 2 * zh_)

    def project(side, rel):
        lhs = G[rows(side * 256, 256), :]
        for j in range(3):
            acc = jnp.dot(lhs, wq[j], preferred_element_type=F32).reshape(2, 2, 4, 2, 8, 256)
            for h in range(2):
                for col in range(2):
                    tiles = [acc[h, cc, yy, col] for yy in range(4) for cc in range(2)]
                    val = jnp.concatenate(tiles, axis=0).astype(BF16)
                    for hd in range(2):
                        QB[hd, h * 2 + col, rows(side * 64, 64), j * 128:(j + 1) * 128] = val[:, hd * 128:(hd + 1) * 128]
        part = rows(side * 64, 64)
        for d in (2, 1, 3, 0):
            head_, pair_ = role(m4(x + d))
            src = QB.at[head_, pl.ds(pair_ * 2, 2), part]
            dst = XR.at[place(zh, zl, pair_, side), x, :, part]
            if d:
                xc[rel, d] = rcopy(src, dst, S_X + rel * 3 + d - 1, xdev[d])
                xc[rel, d].start()
            else:
                own_x[rel] = pltpu.make_async_copy(src, dst, lsem.at[1 + rel])
                own_x[rel].start()

    def first_project():
        wait(fetch_q)
        project(zl, 0)
        start(fetch_o)
        start(fetch_g)
        start(fetch_d)

    gather(first_project)
    project(1 - zl, 1)
    bias_copies[2].start()

    zc, zq = {}, {}
    for rel in range(2):
        side = zl if rel == 0 else 1 - zl
        part = rows(side * 64, 64)
        for d in (0, 1, 3, 2):
            if d:
                xc[rel, d].wait_recv()
            else:
                own_x[rel].wait()
            spot = (place(zh, zl, pair, side), m4(x - d), slice(None), part)
            if rel:
                ref = XR.at[spot + (pl.ds(0, 128),)]
                zq[d] = rcopy(ref, ref, S_ZQ + d, zhpart)
                pl.when(pair == 1)(zq[d].start)
            ref = XR.at[spot + (pl.ds(128, 256),)]
            zc[rel, d] = rcopy(ref, ref, S_ZH + rel * 4 + d, zhpart)
            zc[rel, d].start()
    wg[:, UNITS:UPAD, :] = jnp.zeros((2, UPAD - UNITS, D), BF16)
    wd[UNITS:UPAD, :] = jnp.zeros((UPAD - UNITS, D), BF16)
    own_bias.wait()
    for d in (1, 3, 2):
        bias_copies[d].wait_recv()
    for cp in zc.values():
        cp.wait_recv()
    for cp in zq.values():
        pl.when(pair == 1)(cp.wait_recv)

    ctx = {}
    local = {}
    for d in (2, 1, 3, 0):
        block = m4(x + d)
        heads_out = []
        for col in range(2):
            q = XR[zh, block, col, :, 0:128]
            k1 = XR[0, :, col, :, 128:256].reshape(512, 128)
            k2 = XR[1, :, col, :, 128:256].reshape(512, 128)
            dims = (((1,), (1,)), ((), ()))
            s1 = lax.dot_general(q, k1, dims, preferred_element_type=F32) * SCALE + BV[block, :, 0:512]
            s2 = lax.dot_general(q, k2, dims, preferred_element_type=F32) * SCALE + BV[block, :, 512:1024]
            peak = jnp.maximum(jnp.max(s1, axis=-1, keepdims=True), jnp.max(s2, axis=-1, keepdims=True))
            e1, e2 = jnp.exp(s1 - peak), jnp.exp(s2 - peak)
            total = jnp.sum(e1, axis=-1, keepdims=True) + jnp.sum(e2, axis=-1, keepdims=True)
            v1 = XR[0, :, col, :, 256:384].reshape(512, 128)
            v2 = XR[1, :, col, :, 256:384].reshape(512, 128)
            out = jnp.dot(e1.astype(BF16), v1, preferred_element_type=F32)
            out = out + jnp.dot(e2.astype(BF16), v2, preferred_element_type=F32)
            heads_out.append((out / total).reshape(2, 4, 2, 8, 128))
        tiles = [heads_out[col][zz, yy, cc] for zz in range(2) for cc in range(2) for yy in range(4) for col in range(2)]
        CS[block] = jnp.concatenate(tiles, axis=0).astype(BF16).reshape(2, 8, 16, 128)
        for rel in range(2):
            side = zl if rel == 0 else 1 - zl
            src, dst = CS.at[block, side], CH.at[head, side, pair]
            target = dev(zh_=place(zh, zl, pair, side), x_=block)
            slot = S_CTX + rel * 4 + d
            if d:
                ctx[rel, d] = rcopy(src, dst, slot, target)
                ctx[rel, d].start()
            else:
                local[rel] = pltpu.make_async_copy(src, dst, lsem.at[3 + rel])
                if rel == 0:
                    local[0].start()
                else:
                    ctx[1, 0] = rcopy(src, dst, slot, zhpart)
                    pl.when(pair == 1)(ctx[1, 0].start)
                    pl.when(pair == 0)(local[1].start)
    wait(fetch_o)
    for d in (2, 1, 3):
        for rel in range(2):
            ctx[rel, d].wait_recv()
    local[0].wait()
    pl.when(pair == 1)(ctx[1, 0].wait_recv)
    pl.when(pair == 0)(local[1].wait)

    def out_projection(side):
        @pl.loop(0, 8)
        def _(n):
            lhs = jnp.concatenate([CH[hd, side].reshape(256, 128) for hd in range(2)], axis=1)
            span = pl.ds(pl.multiple_of(n * 512, 512), 512)
            PT[rows(side * 256, 256), span] = jnp.dot(lhs, wo[:, span], preferred_element_type=F32).astype(BF16)

    def add_attended(h, sums):
        part = slice(h * 16, (h + 1) * 16)
        state[part, :] = (cells[part, :].astype(F32) + sums).astype(BF16)
        piece(G, zl, h, c, y)[...] = normalize(state[part, :], gain2[...])

    scatter(out_projection, add_attended)

    def units(side):
        @pl.loop(0, 3)
        def _(n):
            lhs = G[rows(side * 256, 256), :]
            span = rows(n * 256, 256)
            dims = (((1,), (1,)), ((), ()))
            gate = lax.dot_general(lhs, wg[0, span, :], dims, preferred_element_type=F32)
            up = lax.dot_general(lhs, wg[1, span, :], dims, preferred_element_type=F32)
            ACT[rows(side * 256, 256), pl.ds(pl.multiple_of(n * 256, 256), 256)] = (
                gate / (1.0 + jnp.exp(-gate)) * up).astype(BF16)

    def first_units():
        wait(fetch_g)
        units(zl)

    gather(first_units)
    units(1 - zl)
    wait(fetch_d)

    def down_projection(side):
        @pl.loop(0, 8)
        def _(n):
            span = pl.ds(pl.multiple_of(n * 512, 512), 512)
            PT[rows(side * 256, 256), span] = jnp.dot(
                ACT[rows(side * 256, 256), :], wd[:, span], preferred_element_type=F32).astype(BF16)

    def add_feed(h, sums):
        part = slice(h * 16, (h + 1) * 16)
        result[part, :] = (state[part, :].astype(F32) + sums).astype(BF16)

    scatter(down_projection, add_feed)
    for cp in [*bias_copies.values(), *xc.values(), *zc.values()]:
        cp.wait_send()
    for key, cp in ctx.items():
        if key != (1, 0):
            cp.wait_send()

    @pl.when(pair == 1)
    def _():
        for cp in [*zq.values(), ctx[1, 0]]:
            cp.wait_send()


def shards(cells, norm1_gain, w_qkv, row_bias, w_out, norm2_gain, w_gate_up, w_down):
    own = cells.transpose(1, 0, 2).reshape(32, D)
    vmem = pl.BlockSpec(memory_space=pltpu.VMEM)
    hbm = pl.BlockSpec(memory_space=pl.ANY)
    out = jax.ShapeDtypeStruct((32, D), BF16)
    state, result = pl.pallas_call(
        layer,
        out_shape=(out, out),
        in_specs=[vmem, vmem, hbm, hbm, hbm, vmem, hbm, hbm],
        out_specs=(vmem, vmem),
        scratch_shapes=[
            pltpu.VMEM((3, D, 256), BF16),
            pltpu.VMEM((256, D), BF16),
            pltpu.VMEM((2, UPAD, D), BF16),
            pltpu.VMEM((UPAD, D), BF16),
            pltpu.VMEM((512, D), BF16),
            pltpu.VMEM((512, D), BF16),
            pltpu.VMEM((2, 2, 4, 16, D), BF16),
            pltpu.VMEM((2, 4, 16, D), BF16),
            pltpu.VMEM((2, 2, 16, D), BF16),
            pltpu.VMEM((2, 2, 16, D // 2), BF16),
            pltpu.VMEM((4, 128, 1024), F32),
            pltpu.VMEM((2, 4, 128, 384), BF16),
            pltpu.VMEM((2, 4, 2, 128, 384), BF16),
            pltpu.VMEM((4, 2, 8, 16, 128), BF16),
            pltpu.VMEM((2, 2, 2, 8, 16, 128), BF16),
            pltpu.VMEM((512, UPAD), BF16),
            pltpu.SemaphoreType.DMA((N_SEM,)),
            pltpu.SemaphoreType.DMA((N_SEM,)),
            pltpu.SemaphoreType.DMA((36,)),
        ],
        compiler_params=pltpu.CompilerParams(
            collective_id=0, has_side_effects=True, vmem_limit_bytes=60 * 2**20),
        name="layer",
    )(own, norm1_gain.reshape(1, D), w_qkv.transpose(1, 0, 2), row_bias, w_out,
      norm2_gain.reshape(1, D), w_gate_up.transpose(1, 2, 0), w_down)
    return tuple(v.reshape(4, 8, D).transpose(1, 0, 2) for v in (state, result))


def solution(mesh):
    in_specs = (
        P(("row", "tensor"), None, None),
        P(),
        P(None, None, "tensor"),
        P("tensor", "row", None),
        P("tensor", None),
        P(),
        P(None, None, "tensor"),
        P("tensor", None),
    )
    out_specs = (P(("row", "tensor"), None, None), P(("row", "tensor"), None, None))
    return jax.shard_map(shards, mesh=mesh, in_specs=in_specs, out_specs=out_specs, check_vma=False)
```

time: 400 us -> 131 us (0.33)
  waiting for transfers between devices: 302 us -> 0 us
  Pallas kernels: 0 us -> 126 us
  local copies, waits for them, and re-layouts: 39.1 us -> 4.03 us
  matrix products: 32.4 us -> 0 us
  between operations: 14.2 us -> 0.64 us
  other arithmetic: 7.51 us -> 0 us
    all_gather x4 -> x0, waiting for transfers between devices: 178 us -> none  [the longest x1 53.6 us: shards(): lax.all_gather(values_local, 'row', axis=0, tiled=True)]
    pallas_call x0 -> x1, Pallas kernels: none -> 126 us  [shards(): pl.pallas_call(layer, out_shape=(out, out), in_specs=[vmem, vmem, hbm, hb...]
    unnamed x8 -> x0, waiting for transfers between devices: 125 us -> none
    dot_general x6 -> x0, matrix products: 32.4 us -> none  [the longest x1 9.71 us: shards(): jnp.dot(piece.reshape(-1, width), gate_flat, preferred_element_type=jnp.f...]
    unnamed x19 -> x0, local copies, waits for them, and re-layouts: 19.6 us -> none
    reshape x2 -> x0, local copies, waits for them, and re-layouts: 9.72 us -> none  [the longest x1 6.92 us: shards(): piece.reshape(-1, width)]
    all_gather x1 -> x0, local copies, waits for them, and re-layouts: 7.49 us -> none  [shards(): lax.all_gather(normalize(cells, norm1_gain), 'tensor', axis=0, tiled=True)]
    transpose x0 -> x2, local copies, waits for them, and re-layouts: none -> 4.03 us  [the longest x1 2.23 us: shards(): v.reshape(4, 8, D).transpose(1, 0, 2)]
  transfers between devices with their start and end apart: 6 -> 0, of which waited for: 6 -> 0; matrix products, arithmetic and copies ran while one was open for 4% -> 0% of each run, Pallas kernels for 0% -> 0%
where the time goes in v2:
time: 131 us; the launch traced here: 130 us
  Pallas kernels  126 us (96%)
  local copies, waits for them, and re-layouts  4.03 us (3%)
    pallas_call x1, Pallas kernels, shards(): pl.pallas_call(layer, out_shape=(out, out), in_specs=[vmem, vmem, hbm, hb...  126 us

profile of v2, /device:TPU:1, one launch (start us, length us, event | category | flops | bytes accessed | tf_op | source)
XLA Modules:
  0.0 130.4 jit_solution(5388600065550615687)
XLA Ops:
  0.6 1.8 %copy.16 = bf16[4,8,4096]{2,1,0:T(8,128)(2,1)} copy(bf16[4,8,4096]{2,0,1:T(4,128)(2,1)} %bitcast.17) | data formatting | bytes 524288 | tf_op jit(solution)/shard_map/transpose | solution.py:418
  2.4 125.8 %layer.1 = (bf16[32,4096]{1,0:T(8,128)(2,1)}, bf16[32,4096]{1,0:T(8,128)(2,1)}) custom-call(bf16[32,4096]{1,0:T(8,128)(2,1)} %bitcast.16, f32[1,4096]{1,0:T(1,128)} %bitcast.20, bf16[3,4096,256]{2,1,0:T(8,128)(2,1)} %bitcast.15, f32[2,128,1024]{2,1,0:T(8,128)} %bias_hbm.1, bf16[256,4096]{1,0:T(8,128)(2,1)} %wout_hbm.1, f32[1,4096]{1,0:T(1,128)} %bitcast.21, ...), custom_call_target="tpu_custom_call" | custom-call | tf_op jit(solution)/shard_map/layer/pallas_call | solution.py:422
  128.2 2.2 %copy_bitcast_fusion = (bf16[8,4,4096]{2,1,0:T(4,128)(2,1)}, bf16[8,4,4096]{2,1,0:T(4,128)(2,1)}) fusion(bf16[4,8,4096]{2,1,0:T(8,128)(2,1)} %bitcast.19, bf16[4,8,4096]{2,1,0:T(8,128)(2,1)} %bitcast.18), kind=kLoop, calls=%fused_computation | loop fusion | bytes 1048576 | tf_op jit(solution)/shard_map/transpose | solution.py:453

commit v3 on v2

--- a/solution.py
+++ b/solution.py
@@ -17,9 +17,9 @@
 SCALE = 1.0 / math.sqrt(128)
 
 S_BIAS, S_X, S_ZH, S_ZQ, S_CTX = 0, 3, 9, 17, 21
-AG_Z, AG_Y, AG_FWD, AG_OWN, AG_NEAR, AG_FAR = 29, 39, 43, 47, 49, 57
-RS_C, RS_Z, RS_Y, RS_FWD = 67, 83, 91, 95
-N_SEM = 99
+AG_Z, AG_Y, AG_FWD, AG_OWN, AG_NEAR, AG_FAR = 29, 43, 51, 55, 57, 69
+RS_C, RS_Z, RS_Y, RS_FWD = 83, 99, 115, 123
+N_SEM = 127
 
 
 def rows(start, count):
@@ -99,7 +99,11 @@
 
     pl.semaphore_wait(barrier, len(peers))
 
-    low, high = pl.ds(0, D // 2), pl.ds(D // 2, D // 2)
+    lanes = (pl.ds(0, D // 2), pl.ds(D // 2, D // 2))
+    turns = ((0, 1), (1, 3), (1, 1), (0, 3))
+
+    def first(d):
+        return d // 2
 
     def gather(middle):
         sends = []
@@ -110,57 +114,59 @@
             sends.append(cp)
             return cp
 
-        def mine(h):
+        zs, ys, fwd, near, far = {}, {}, {}, [], []
+        steps = [(h, d, first(d)) for h, d in turns] + [(h, d, 1 - first(d)) for h, d in turns]
+        ahead = [(h, 2, first(d)) for h, d in turns]
+
+        def own(h):
             return piece(G, zl, h, c, y)
 
-        zs, ys, near, far = {}, {}, [], []
-
-        def hop(h, d):
-            ys[h, d] = send(mine(h), AG_Y + h * 2 + d // 2, ydev[d])
-
-        def arrive(h, d):
-            ys[h, d].wait_recv()
-            src = piece(G, zl, h, c, m4(y - d))
-            zs[h, d] = send(src, AG_Z + h * 5 + d // 2 + 1, zdev[h])
-            near.append(send(src, AG_NEAR + h * 4 + d // 2, sib))
-
-        hop(0, 1)
-        hop(1, 3)
-        for h in range(2):
-            zs[h, 0] = send(mine(h), AG_Z + h * 5, zdev[h])
-            near.append(send(mine(h), AG_OWN + h, sib))
-        arrive(0, 1)
-        hop(1, 1)
-        arrive(1, 3)
-        hop(0, 3)
-        fwd = {}
-
-        def forward(h, d):
-            lanes = low if d == 1 else high
-            fwd[h, d] = send(piece(G, zl, h, c, m4(y - d)).at[:, lanes], AG_FWD + h * 2 + d // 2, ydev[d])
-
-        arrive(1, 1)
-        forward(0, 1)
-        forward(1, 1)
-        arrive(0, 3)
-        forward(1, 3)
-        forward(0, 3)
-        for d in (1, 3):
-            for h in range(2):
-                fwd[h, d].wait_recv()
-                src = piece(G, zl, h, c, m4(y + 2)).at[:, low if d == 1 else high]
-                zs[h, d + 3] = send(src, AG_Z + h * 5 + 3 + d // 2, zdev[h])
-                near.append(send(src, AG_NEAR + h * 4 + 2 + d // 2, sib))
+        def hop(h, d, i):
+            ys[h, d, i] = send(own(h).at[:, lanes[i]], AG_Y + h * 4 + first(d) * 2 + i, ydev[d])
+
+        def spot(zl_, h, d, i):
+            return piece(G, zl_, h, c, m4(y - d)).at[:, lanes[i]]
+
+        def spread(h, d, i):
+            src = spot(zl, h, d, i)
+            zs[h, d, i] = send(src, AG_Z + h * 7 + d * 2 + i - 1, zdev[h])
+            near.append(send(src, AG_NEAR + h * 6 + d * 2 + i - 2, sib))
+
+        def arrive(h, d, i):
+            ys[h, d, i].wait_recv()
+            if i == first(d):
+                fwd[h, i] = send(spot(zl, h, d, i), AG_FWD + h * 2 + i, ydev[d])
+            spread(h, d, i)
+
+        def cross(h, d, i):
+            zs[h, d, i].wait_recv()
+            far.append(send(spot(1 - zl, h, d, i), AG_FAR + h * 7 + d * 2 + i - 1, sib))
+
+        for step in steps[:4]:
+            hop(*step)
+        for h in range(2):
+            zs[h, 0] = send(own(h), AG_Z + h * 7, zdev[h])
+        for step in steps[4:]:
+            hop(*step)
+        for h in range(2):
+            near.append(send(own(h), AG_OWN + h, sib))
+        for step in steps[:4]:
+            arrive(*step)
+        for h in range(2):
+            zs[h, 0].wait_recv()
+            far.append(send(piece(G, 1 - zl, h, c, y), AG_FAR + h * 7, sib))
+        for step in steps[4:]:
+            arrive(*step)
+        for step in steps[:4]:
+            cross(*step)
+        for h, d, i in ahead:
+            fwd[h, i].wait_recv()
+            spread(h, d, i)
         for cp in near:
             cp.wait_recv()
         middle()
-        for i, d in enumerate((0, 1, 3, 4, 6)):
-            for h in range(2):
-                zs[h, d].wait_recv()
-                src = piece(G, 1 - zl, h, c, m4(y - d if d < 4 else y + 2))
-                if d > 3:
-                    src = src.at[:, low if d == 4 else high]
-                far.append(send(src, AG_FAR + h * 5 + i, sib))
+        for step in steps[4:] + ahead:
+            cross(*step)
         for cp in far:
             cp.wait_recv()
         for cp in sends:
@@ -181,7 +187,7 @@
                 total = total + other[...].astype(F32)
             slot[...] = total.astype(BF16)
 
-        order = [(h, d) for d in (2, 1, 3, 0) for h in range(2)]
+        order = [(0, 2), (1, 2), *turns, (0, 0), (1, 0)]
         cs, zs, ys, fwd = {}, {}, {}, {}
 
         def share(zrel):
@@ -194,52 +200,59 @@
             cs[h, d].wait_recv()
             add(RC.at[zrel, h, d], piece(PT, zl if zrel == 0 else 1 - zl, h, c, m4(y + d)))
 
-        def cross(h, d):
-            zs[h, d] = send(RC.at[1, h, d], RZ.at[h, d], RS_Z + h * 4 + d, zdev[h])
+        def cross(h, d, i):
+            zs[h, d, i] = send(RC.at[1, h, d, :, lanes[i]], RZ.at[h, d, :, lanes[i]],
+                               RS_Z + h * 8 + d * 2 + i, zdev[h])
+
+        def hop(h, d, i, *others):
+            zs[h, d, i].wait_recv()
+            slot = RC.at[0, h, d, :, lanes[i]]
+            add(slot, RZ.at[h, d, :, lanes[i]], *others)
+            ys[h, d, i] = send(slot, RY.at[h, first(d), :, lanes[i]], RS_Y + h * 4 + first(d) * 2 + i, ydev[d])
 
         produce(1 - zl)
         share(1)
         for h in range(2):
             pair_up(1, h, 2)
-            cross(h, 2)
-        for h, d in order[2:]:
+            for i in range(2):
+                cross(h, 2, i)
+        for h, d in turns:
             pair_up(1, h, d)
-        cross(0, 1)
-        cross(1, 3)
+            cross(h, d, 1 - first(d))
+        for h, d in turns:
+            cross(h, d, first(d))
+        for h in range(2):
+            pair_up(1, h, 0)
+            for i in range(2):
+                cross(h, 0, i)
         produce(zl)
         share(0)
         for h in range(2):
-            zs[h, 2].wait_send()
-            cross(h, 3 if h == 0 else 1)
-        for h in range(2):
             pair_up(0, h, 2)
-            zs[h, 2].wait_recv()
-            add(RC.at[0, h, 2], RZ.at[h, 2])
-            for d, lanes in ((1, low), (3, high)):
-                fwd[h, d] = send(RC.at[0, h, 2, :, lanes], RF.at[h, d // 2], RS_FWD + h * 2 + d // 2, ydev[d])
-        for h, d in order[2:]:
+            for i, d in ((0, 1), (1, 3)):
+                zs[h, 2, i].wait_recv()
+                slot = RC.at[0, h, 2, :, lanes[i]]
+                add(slot, RZ.at[h, 2, :, lanes[i]])
+                fwd[h, i] = send(slot, RF.at[h, i], RS_FWD + h * 2 + i, ydev[d])
+        for h, d in turns:
             pair_up(0, h, d)
-        for h in range(2):
-            zs[h, 1 if h == 0 else 3].wait_send()
-            cross(h, 0)
-        for h, d in ((0, 1), (1, 3), (0, 3), (1, 1)):
-            fwd[h, d].wait_recv()
-            zs[h, d].wait_recv()
-            first, second = (low, high) if d == 1 else (high, low)
-            slot = RC.at[0, h, d]
-            add(slot.at[:, first], RZ.at[h, d, :, first], RF.at[h, d // 2])
-            add(slot.at[:, second], RZ.at[h, d, :, second])
-            ys[h, d] = send(slot, RY.at[h, d // 2], RS_Y + h * 2 + d // 2, ydev[d])
-        for h in range(2):
-            zs[h, 0].wait_recv()
+            hop(h, d, 1 - first(d))
+        for h, d in turns:
+            fwd[h, first(d)].wait_recv()
+            hop(h, d, first(d), RF.at[h, first(d)])
+        for h in range(2):
+            pair_up(0, h, 0)
+        for h in range(2):
+            for i in range(2):
+                zs[h, 0, i].wait_recv()
             sums = RC[0, h, 0].astype(F32) + RZ[h, 0].astype(F32)
             for d in (1, 3):
-                ys[h, d].wait_recv()
-                sums = sums + RY[h, d // 2].astype(F32)
+                for i in range(2):
+                    ys[h, d, i].wait_recv()
+                sums = sums + RY[h, first(d)].astype(F32)
             finish(h, sums)
         for cp in sends:
-            if not any(cp is done for done in (zs[0, 2], zs[1, 2], zs[0, 1], zs[1, 3])):
-                cp.wait_send()
+            cp.wait_send()
 
     own_bias.start()
     bias_copies = {d: rcopy(bias_hbm.at[role(m4(x + d))[0]], BV.at[x], S_BIAS + d - 1, xdev[d]) for d in (1, 2, 3)}

time: 131 us -> 121 us (0.924)
  Pallas kernels: 126 us -> 117 us
    pallas_call x1, Pallas kernels: 126 us -> 117 us  [shards(): pl.pallas_call(layer, out_shape=(out, out), in_specs=[vmem, vmem, hbm, hb...]
where the time goes in v3:
time: 121 us
  Pallas kernels  117 us (97%)
  local copies, waits for them, and re-layouts  4.03 us (3%)
    pallas_call x1, Pallas kernels, shards(): pl.pallas_call(layer, out_shape=(out, out), in_specs=[vmem, vmem, hbm, hb...  117 us

profile of v3, /device:TPU:1, one launch (start us, length us, event | category | flops | bytes accessed | tf_op | source)
XLA Modules:
  0.0 121.2 jit_solution(3773104631378557331)
XLA Ops:
  0.6 1.8 %copy.16 = bf16[4,8,4096]{2,1,0:T(8,128)(2,1)} copy(bf16[4,8,4096]{2,0,1:T(4,128)(2,1)} %bitcast.17) | data formatting | bytes 524288 | tf_op jit(solution)/shard_map/transpose | solution.py:431
  2.4 116.5 %layer.1 = (bf16[32,4096]{1,0:T(8,128)(2,1)}, bf16[32,4096]{1,0:T(8,128)(2,1)}) custom-call(bf16[32,4096]{1,0:T(8,128)(2,1)} %bitcast.16, f32[1,4096]{1,0:T(1,128)} %bitcast.20, bf16[3,4096,256]{2,1,0:T(8,128)(2,1)} %bitcast.15, f32[2,128,1024]{2,1,0:T(8,128)} %bias_hbm.1, bf16[256,4096]{1,0:T(8,128)(2,1)} %wout_hbm.1, f32[1,4096]{1,0:T(1,128)} %bitcast.21, ...), custom_call_target="tpu_custom_call" | custom-call | tf_op jit(solution)/shard_map/layer/pallas_call | solution.py:435
  118.9 2.2 %copy_bitcast_fusion = (bf16[8,4,4096]{2,1,0:T(4,128)(2,1)}, bf16[8,4,4096]{2,1,0:T(4,128)(2,1)}) fusion(bf16[4,8,4096]{2,1,0:T(8,128)(2,1)} %bitcast.19, bf16[4,8,4096]{2,1,0:T(8,128)(2,1)} %bitcast.18), kind=kLoop, calls=%fused_computation | loop fusion | bytes 1048576 | tf_op jit(solution)/shard_map/transpose | solution.py:466

commit v4 on v3

--- a/solution.py
+++ b/solution.py
@@ -18,8 +18,8 @@
 
 S_BIAS, S_X, S_ZH, S_ZQ, S_CTX = 0, 3, 9, 17, 21
 AG_Z, AG_Y, AG_FWD, AG_OWN, AG_NEAR, AG_FAR = 29, 43, 51, 55, 57, 69
-RS_C, RS_Z, RS_Y, RS_FWD = 83, 99, 115, 123
-N_SEM = 127
+RS_C, RS_Z, RS_Y, RS_FWD = 83, 115, 131, 139
+N_SEM = 143
 
 
 def rows(start, count):
@@ -33,7 +33,7 @@
 
 
 def layer(cells, gain1, wqkv_hbm, bias_hbm, wout_hbm, gain2, wgu_hbm, wdown_hbm, state, result,
-          wq, wo, wg, wd, G, PT, RC, RZ, RY, RF, BV, QB, XR, CS, CH, ACT, ssem, rsem, lsem):
+          wq, wo, wg, wd, mix, own, G, PT, RC, RZ, RY, RF, BV, QB, XR, CS, CH, ACT, ssem, rsem, lsem):
     r = lax.axis_index("row")
     t = lax.axis_index("tensor")
     zh, x = r // 4, lax.rem(r, 4)
@@ -94,8 +94,16 @@
     for target in peers:
         pl.semaphore_signal(barrier, inc=1, device_id=target, device_id_type=MESH)
 
+    @pl.loop(0, D // 128)
+    def _(n):
+        lane = pl.ds(pl.multiple_of(n * 128, 128), 128)
+        for i in range(8):
+            mix[i * 4:(i + 1) * 4, :] = cells[i, :, lane].astype(F32)
+        for col in range(4):
+            own[col * 8:(col + 1) * 8, lane] = mix[pl.ds(col, 8, stride=4), :]
+
     for h in range(2):
-        piece(G, zl, h, c, y)[...] = normalize(cells[h * 16:(h + 1) * 16, :], gain1[...])
+        piece(G, zl, h, c, y)[...] = normalize(own[h * 16:(h + 1) * 16, :], gain1[...])
 
     pl.semaphore_wait(barrier, len(peers))
 
@@ -164,9 +172,13 @@
             spread(h, d, i)
         for cp in near:
             cp.wait_recv()
-        middle()
-        for step in steps[4:] + ahead:
+        middle[0]()
+        for step in steps[4:]:
             cross(*step)
+        middle[1]()
+        for step in ahead:
+            cross(*step)
+        middle[2]()
         for cp in far:
             cp.wait_recv()
         for cp in sends:
@@ -192,56 +204,56 @@
 
         def share(zrel):
             side = zl if zrel == 0 else 1 - zl
-            for h, d in order:
-                cs[h, d] = send(piece(PT, side, h, 1 - c, m4(y + d)), RC.at[zrel, h, d],
-                                RS_C + zrel * 8 + h * 4 + d, sib)
-
-        def pair_up(zrel, h, d):
-            cs[h, d].wait_recv()
-            add(RC.at[zrel, h, d], piece(PT, zl if zrel == 0 else 1 - zl, h, c, m4(y + d)))
+            for i in range(2):
+                produce(side, i)
+                for h, d in order:
+                    cs[h, d, i] = send(piece(PT, side, h, 1 - c, m4(y + d)).at[:, lanes[i]],
+                                       RC.at[zrel, h, d, :, lanes[i]], RS_C + zrel * 16 + h * 8 + d * 2 + i, sib)
+
+        def pair_up(zrel, h, d, i):
+            cs[h, d, i].wait_recv()
+            side = zl if zrel == 0 else 1 - zl
+            add(RC.at[zrel, h, d, :, lanes[i]], piece(PT, side, h, c, m4(y + d)).at[:, lanes[i]])
 
         def cross(h, d, i):
+            pair_up(1, h, d, i)
             zs[h, d, i] = send(RC.at[1, h, d, :, lanes[i]], RZ.at[h, d, :, lanes[i]],
                                RS_Z + h * 8 + d * 2 + i, zdev[h])
 
         def hop(h, d, i, *others):
+            pair_up(0, h, d, i)
             zs[h, d, i].wait_recv()
             slot = RC.at[0, h, d, :, lanes[i]]
             add(slot, RZ.at[h, d, :, lanes[i]], *others)
             ys[h, d, i] = send(slot, RY.at[h, first(d), :, lanes[i]], RS_Y + h * 4 + first(d) * 2 + i, ydev[d])
 
-        produce(1 - zl)
         share(1)
-        for h in range(2):
-            pair_up(1, h, 2)
-            for i in range(2):
+        for i, d in ((0, 3), (1, 1)):
+            for h in range(2):
                 cross(h, 2, i)
-        for h, d in turns:
-            pair_up(1, h, d)
-            cross(h, d, 1 - first(d))
+            for h in range(2):
+                cross(h, d, i)
         for h, d in turns:
             cross(h, d, first(d))
         for h in range(2):
-            pair_up(1, h, 0)
             for i in range(2):
                 cross(h, 0, i)
-        produce(zl)
         share(0)
-        for h in range(2):
-            pair_up(0, h, 2)
-            for i, d in ((0, 1), (1, 3)):
+        for i, d in ((0, 1), (1, 3)):
+            for h in range(2):
+                pair_up(0, h, 2, i)
                 zs[h, 2, i].wait_recv()
                 slot = RC.at[0, h, 2, :, lanes[i]]
                 add(slot, RZ.at[h, 2, :, lanes[i]])
                 fwd[h, i] = send(slot, RF.at[h, i], RS_FWD + h * 2 + i, ydev[d])
         for h, d in turns:
-            pair_up(0, h, d)
             hop(h, d, 1 - first(d))
         for h, d in turns:
             fwd[h, first(d)].wait_recv()
             hop(h, d, first(d), RF.at[h, first(d)])
         for h in range(2):
-            pair_up(0, h, 0)
+            for i in range(2):
+                pair_up(0, h, 0, i)
         for h in range(2):
             for i in range(2):
                 zs[h, 0, i].wait_recv()
@@ -256,24 +268,25 @@
 
     own_bias.start()
     bias_copies = {d: rcopy(bias_hbm.at[role(m4(x + d))[0]], BV.at[x], S_BIAS + d - 1, xdev[d]) for d in (1, 2, 3)}
-    bias_copies[1].start()
-    bias_copies[3].start()
+    for d in (1, 3):
+        bias_copies[d].start()
 
     xc, own_x = {}, {}
 
     def place(zh_, zl_, pair_, part):
         return zh_ + pair_ * lax.rem(zl_ + part, 2) * (1 - 2 * zh_)
 
-    def project(side, rel):
+    def project(side, j):
         lhs = G[rows(side * 256, 256), :]
-        for j in range(3):
-            acc = jnp.dot(lhs, wq[j], preferred_element_type=F32).reshape(2, 2, 4, 2, 8, 256)
-            for h in range(2):
-                for col in range(2):
-                    tiles = [acc[h, cc, yy, col] for yy in range(4) for cc in range(2)]
-                    val = jnp.concatenate(tiles, axis=0).astype(BF16)
-                    for hd in range(2):
-                        QB[hd, h * 2 + col, rows(side * 64, 64), j * 128:(j + 1) * 128] = val[:, hd * 128:(hd + 1) * 128]
+        acc = jnp.dot(lhs, wq[j], preferred_element_type=F32).reshape(2, 2, 4, 2, 8, 256)
+        for h in range(2):
+            for col in range(2):
+                tiles = [acc[h, cc, yy, col] for yy in range(4) for cc in range(2)]
+                val = jnp.concatenate(tiles, axis=0).astype(BF16)
+                for hd in range(2):
+                    QB[hd, h * 2 + col, rows(side * 64, 64), j * 128:(j + 1) * 128] = val[:, hd * 128:(hd + 1) * 128]
+
+    def ship(side, rel):
         part = rows(side * 64, 64)
         for d in (2, 1, 3, 0):
             head_, pair_ = role(m4(x + d))
@@ -286,20 +299,19 @@
                 own_x[rel] = pltpu.make_async_copy(src, dst, lsem.at[1 + rel])
                 own_x[rel].start()
 
-    def first_project():
-        wait(fetch_q)
-        project(zl, 0)
+    def last_step():
+        project(zl, 2)
+        ship(zl, 0)
         start(fetch_o)
         start(fetch_g)
         start(fetch_d)
 
-    gather(first_project)
-    project(1 - zl, 1)
-    bias_copies[2].start()
+    wait(fetch_q)
+    gather([functools.partial(project, zl, 0), functools.partial(project, zl, 1), last_step])
 
     zc, zq = {}, {}
-    for rel in range(2):
-        side = zl if rel == 0 else 1 - zl
+
+    def pass_on(side, rel):
         part = rows(side * 64, 64)
         for d in (0, 1, 3, 2):
             if d:
@@ -314,10 +326,17 @@
             ref = XR.at[spot + (pl.ds(128, 256),)]
             zc[rel, d] = rcopy(ref, ref, S_ZH + rel * 4 + d, zhpart)
             zc[rel, d].start()
+
+    for j in range(3):
+        project(1 - zl, j)
+    ship(1 - zl, 1)
+    bias_copies[2].start()
+    pass_on(zl, 0)
+    pass_on(1 - zl, 1)
     wg[:, UNITS:UPAD, :] = jnp.zeros((2, UPAD - UNITS, D), BF16)
     wd[UNITS:UPAD, :] = jnp.zeros((UPAD - UNITS, D), BF16)
     own_bias.wait()
-    for d in (1, 3, 2):
+    for d in (1, 3):
         bias_copies[d].wait_recv()
     for cp in zc.values():
         cp.wait_recv()
@@ -326,9 +345,11 @@
 
     ctx = {}
     local = {}
-    for d in (2, 1, 3, 0):
+    for d in (1, 3, 0, 2):
         block = m4(x + d)
         heads_out = []
+        if d == 2:
+            bias_copies[2].wait_recv()
         for col in range(2):
             q = XR[zh, block, col, :, 0:128]
             k1 = XR[0, :, col, :, 128:256].reshape(512, 128)
@@ -370,8 +391,8 @@
     pl.when(pair == 1)(ctx[1, 0].wait_recv)
     pl.when(pair == 0)(local[1].wait)
 
-    def out_projection(side):
-        @pl.loop(0, 8)
+    def out_projection(side, i):
+        @pl.loop(i * 4, i * 4 + 4)
         def _(n):
             lhs = jnp.concatenate([CH[hd, side].reshape(256, 128) for hd in range(2)], axis=1)
             span = pl.ds(pl.multiple_of(n * 512, 512), 512)
@@ -379,32 +400,42 @@
 
     def add_attended(h, sums):
         part = slice(h * 16, (h + 1) * 16)
-        state[part, :] = (cells[part, :].astype(F32) + sums).astype(BF16)
-        piece(G, zl, h, c, y)[...] = normalize(state[part, :], gain2[...])
+        own[part, :] = (own[part, :] + sums).astype(BF16).astype(F32)
+        piece(G, zl, h, c, y)[...] = normalize(own[part, :], gain2[...])
 
     scatter(out_projection, add_attended)
 
-    def units(side):
-        @pl.loop(0, 3)
+    def units(side, n):
+        lhs = G[rows(side * 256, 256), :]
+        span = rows(n * 256, 256)
+        dims = (((1,), (1,)), ((), ()))
+        gate = lax.dot_general(lhs, wg[0, span, :], dims, preferred_element_type=F32)
+        up = lax.dot_general(lhs, wg[1, span, :], dims, preferred_element_type=F32)
+        ACT[rows(side * 256, 256), pl.ds(pl.multiple_of(n * 256, 256), 256)] = (
+            gate / (1.0 + jnp.exp(-gate)) * up).astype(BF16)
+
+    def unmix(out):
+        @pl.loop(0, D // 128)
         def _(n):
-            lhs = G[rows(side * 256, 256), :]
-            span = rows(n * 256, 256)
-            dims = (((1,), (1,)), ((), ()))
-            gate = lax.dot_general(lhs, wg[0, span, :], dims, preferred_element_type=F32)
-            up = lax.dot_general(lhs, wg[1, span, :], dims, preferred_element_type=F32)
-            ACT[rows(side * 256, 256), pl.ds(pl.multiple_of(n * 256, 256), 256)] = (
-                gate / (1.0 + jnp.exp(-gate)) * up).astype(BF16)
-
-    def first_units():
-        wait(fetch_g)
-        units(zl)
-
-    gather(first_units)
-    units(1 - zl)
+            lane = pl.ds(pl.multiple_of(n * 128, 128), 128)
+            for col in range(4):
+                mix[pl.ds(col, 8, stride=4), :] = own[col * 8:(col + 1) * 8, lane]
+            for i in range(8):
+                out[i, :, lane] = mix[i * 4:(i + 1) * 4, :].astype(BF16)
+
+    wait(fetch_g)
+    gather([functools.partial(units, zl, n) for n in range(3)])
+
+    unmix(state)
+
+    @pl.loop(0, 3)
+    def _(n):
+        units(1 - zl, n)
+
     wait(fetch_d)
 
-    def down_projection(side):
-        @pl.loop(0, 8)
+    def down_projection(side, i):
+        @pl.loop(i * 4, i * 4 + 4)
         def _(n):
             span = pl.ds(pl.multiple_of(n * 512, 512), 512)
             PT[rows(side * 256, 256), span] = jnp.dot(
@@ -412,9 +443,10 @@
 
     def add_feed(h, sums):
         part = slice(h * 16, (h + 1) * 16)
-        result[part, :] = (state[part, :].astype(F32) + sums).astype(BF16)
+        own[part, :] = own[part, :] + sums
 
     scatter(down_projection, add_feed)
+    unmix(result)
     for cp in [*bias_copies.values(), *xc.values(), *zc.values()]:
         cp.wait_send()
     for key, cp in ctx.items():
@@ -428,11 +460,10 @@
 
 
 def shards(cells, norm1_gain, w_qkv, row_bias, w_out, norm2_gain, w_gate_up, w_down):
-    own = cells.transpose(1, 0, 2).reshape(32, D)
     vmem = pl.BlockSpec(memory_space=pltpu.VMEM)
     hbm = pl.BlockSpec(memory_space=pl.ANY)
-    out = jax.ShapeDtypeStruct((32, D), BF16)
-    state, result = pl.pallas_call(
+    out = jax.ShapeDtypeStruct(cells.shape, BF16)
+    return tuple(pl.pallas_call(
         layer,
         out_shape=(out, out),
         in_specs=[vmem, vmem, hbm, hbm, hbm, vmem, hbm, hbm],
@@ -442,6 +473,8 @@
             pltpu.VMEM((256, D), BF16),
             pltpu.VMEM((2, UPAD, D), BF16),
             pltpu.VMEM((UPAD, D), BF16),
+            pltpu.VMEM((32, 128), F32),
+            pltpu.VMEM((32, D), F32),
             pltpu.VMEM((512, D), BF16),
             pltpu.VMEM((512, D), BF16),
             pltpu.VMEM((2, 2, 4, 16, D), BF16),
@@ -461,9 +494,8 @@
         compiler_params=pltpu.CompilerParams(
             collective_id=0, has_side_effects=True, vmem_limit_bytes=60 * 2**20),
         name="layer",
-    )(own, norm1_gain.reshape(1, D), w_qkv.transpose(1, 0, 2), row_bias, w_out,
-      norm2_gain.reshape(1, D), w_gate_up.transpose(1, 2, 0), w_down)
-    return tuple(v.reshape(4, 8, D).transpose(1, 0, 2) for v in (state, result))
+    )(cells, norm1_gain.reshape(1, D), w_qkv.transpose(1, 0, 2), row_bias, w_out,
+      norm2_gain.reshape(1, D), w_gate_up.transpose(1, 2, 0), w_down))
 
 
 def solution(mesh):

time: 121 us -> 120 us (level); the launches traced: 121 us -> 118 us
  Pallas kernels: 117 us -> 114 us
    transpose x2 -> x0, local copies, waits for them, and re-layouts: 4.03 us -> none  [the longest x1 2.23 us: shards(): v.reshape(4, 8, D).transpose(1, 0, 2)]
    unnamed x0 -> x2, local copies, waits for them, and re-layouts: none -> 3.49 us
    pallas_call x1, Pallas kernels: 117 us -> 114 us  [shards(): pl.pallas_call(layer, out_shape=(out, out), in_specs=[vmem, vmem, hbm, hb...]
where the time goes in v4:
time: 120 us; the launch traced here: 118 us
  Pallas kernels  114 us (95%)
  local copies, waits for them, and re-layouts  3.49 us (3%)
    pallas_call x1, Pallas kernels, shards(): pl.pallas_call(layer, out_shape=(out, out), in_specs=[vmem, vmem, hbm, hb...  114 us
    unnamed x2, local copies, waits for them, and re-layouts  3.49 us

profile of v4, /device:TPU:1, one launch (start us, length us, event | category | flops | bytes accessed | tf_op | source)
XLA Modules:
  0.0 118.4 jit_solution(6775036473584444408)
XLA Ops:
  0.6 114.2 %layer.1 = (bf16[8,4,4096]{2,1,0:T(4,128)(2,1)}, bf16[8,4,4096]{2,1,0:T(4,128)(2,1)}) custom-call(bf16[8,4,4096]{2,1,0:T(4,128)(2,1)} %cells.1, f32[1,4096]{1,0:T(1,128)} %bitcast.6, bf16[3,4096,256]{2,1,0:T(8,128)(2,1)} %bitcast.5, f32[2,128,1024]{2,1,0:T(8,128)} %bias_hbm.1, bf16[256,4096]{1,0:T(8,128)(2,1)} %wout_hbm.1, f32[1,4096]{1,0:T(1,128)} %bitcast.7, ...), custom_call_target="tpu_custom_call" | custom-call | tf_op jit(solution)/shard_map/layer/pallas_call | solution.py:466
  114.9 1.7 %copy.12 = bf16[8,4,4096]{2,1,0:T(4,128)(2,1)} copy(bf16[8,4,4096]{2,1,0:T(4,128)(2,1)} %get-tuple-element.4) | data formatting | bytes 524288
  116.6 1.7 %copy.13 = bf16[8,4,4096]{2,1,0:T(4,128)(2,1)} copy(bf16[8,4,4096]{2,1,0:T(4,128)(2,1)} %get-tuple-element.5) | data formatting | bytes 524288

commit v5 on v4

--- a/solution.py
+++ b/solution.py
@@ -414,19 +414,10 @@
         ACT[rows(side * 256, 256), pl.ds(pl.multiple_of(n * 256, 256), 256)] = (
             gate / (1.0 + jnp.exp(-gate)) * up).astype(BF16)
 
-    def unmix(out):
-        @pl.loop(0, D // 128)
-        def _(n):
-            lane = pl.ds(pl.multiple_of(n * 128, 128), 128)
-            for col in range(4):
-                mix[pl.ds(col, 8, stride=4), :] = own[col * 8:(col + 1) * 8, lane]
-            for i in range(8):
-                out[i, :, lane] = mix[i * 4:(i + 1) * 4, :].astype(BF16)
-
     wait(fetch_g)
     gather([functools.partial(units, zl, n) for n in range(3)])
 
-    unmix(state)
+    state[...] = own[...].astype(BF16)
 
     @pl.loop(0, 3)
     def _(n):
@@ -443,10 +434,9 @@
 
     def add_feed(h, sums):
         part = slice(h * 16, (h + 1) * 16)
-        own[part, :] = own[part, :] + sums
+        result[part, :] = (own[part, :] + sums).astype(BF16)
 
     scatter(down_projection, add_feed)
-    unmix(result)
     for cp in [*bias_copies.values(), *xc.values(), *zc.values()]:
         cp.wait_send()
     for key, cp in ctx.items():
@@ -462,8 +452,8 @@
 def shards(cells, norm1_gain, w_qkv, row_bias, w_out, norm2_gain, w_gate_up, w_down):
     vmem = pl.BlockSpec(memory_space=pltpu.VMEM)
     hbm = pl.BlockSpec(memory_space=pl.ANY)
-    out = jax.ShapeDtypeStruct(cells.shape, BF16)
-    return tuple(pl.pallas_call(
+    out = jax.ShapeDtypeStruct((32, D), BF16)
+    state, result = pl.pallas_call(
         layer,
         out_shape=(out, out),
         in_specs=[vmem, vmem, hbm, hbm, hbm, vmem, hbm, hbm],
@@ -495,7 +485,8 @@
             collective_id=0, has_side_effects=True, vmem_limit_bytes=60 * 2**20),
         name="layer",
     )(cells, norm1_gain.reshape(1, D), w_qkv.transpose(1, 0, 2), row_bias, w_out,
-      norm2_gain.reshape(1, D), w_gate_up.transpose(1, 2, 0), w_down))
+      norm2_gain.reshape(1, D), w_gate_up.transpose(1, 2, 0), w_down)
+    return tuple(v.reshape(4, 8, D).transpose(1, 0, 2) for v in (state, result))
 
 
 def solution(mesh):

time: 120 us -> 119 us (level)
  local copies, waits for them, and re-layouts: 3.49 us -> 2.23 us
    unnamed x2 -> x0, local copies, waits for them, and re-layouts: 3.49 us -> none
    transpose x0 -> x1, local copies, waits for them, and re-layouts: none -> 2.23 us  [shards(): v.reshape(4, 8, D).transpose(1, 0, 2)]
where the time goes in v5:
time: 119 us; the launch traced here: 116 us
  Pallas kernels  114 us (96%)
  local copies, waits for them, and re-layouts  2.23 us (2%)
    pallas_call x1, Pallas kernels, shards(): pl.pallas_call(layer, out_shape=(out, out), in_specs=[vmem, vmem, hbm, hb...  114 us

profile of v5, /device:TPU:1, one launch (start us, length us, event | category | flops | bytes accessed | tf_op | source)
XLA Modules:
  0.0 116.4 jit_solution(14778047433175255088)
XLA Ops:
  0.6 113.6 %layer.1 = (bf16[32,4096]{1,0:T(8,128)(2,1)}, bf16[32,4096]{1,0:T(8,128)(2,1)}) custom-call(bf16[8,4,4096]{2,1,0:T(4,128)(2,1)} %cells.1, f32[1,4096]{1,0:T(1,128)} %bitcast.14, bf16[3,4096,256]{2,1,0:T(8,128)(2,1)} %bitcast.11, f32[2,128,1024]{2,1,0:T(8,128)} %bias_hbm.1, bf16[256,4096]{1,0:T(8,128)(2,1)} %wout_hbm.1, f32[1,4096]{1,0:T(1,128)} %bitcast.15, ...), custom_call_target="tpu_custom_call" | custom-call | tf_op jit(solution)/shard_map/layer/pallas_call | solution.py:456
  114.2 2.2 %copy_bitcast_fusion = (bf16[8,4,4096]{2,1,0:T(4,128)(2,1)}, bf16[8,4,4096]{2,1,0:T(4,128)(2,1)}) fusion(bf16[4,8,4096]{2,1,0:T(8,128)(2,1)} %bitcast.13, bf16[4,8,4096]{2,1,0:T(8,128)(2,1)} %bitcast.12), kind=kLoop, calls=%fused_computation | loop fusion | bytes 1048576 | tf_op jit(solution)/shard_map/transpose | solution.py:489
